TPU v7x, 32 devices: a whole 2x2x4 slice. The times are simulated.
32 devices in a mesh: dp: 16 (over z, y, x), grp: 2 (over core).
Axes of the slice: x: 2, y: 2, z: 4, core: 2. Of those that a mesh axis runs over, the one named last changes fastest.
Arguments:
- embeds: bfloat16 [8192, 1024], P(('dp', 'grp')), may hold values from -7 to 7
- quality: float32 [8192], P(('dp', 'grp')), may hold values from 0.5 to 2
- domain_ids: int32 [8192], P(('dp', 'grp')), may hold values from 0 to 15, as said below
- domain_weight: float32 [16], replicated, may hold values from 0.5 to 2
- dest: int32 [8192], P(('dp', 'grp')), may hold values from 0 to 31, as said below
- counts: int32 [32], P(('dp', 'grp')), may hold values from 192 to 256, as said below
- winners: int32 [4], replicated, may hold values from 0 to 8191, as said below
Outputs:
- relaid: bfloat16 [16384, 1024], P(('dp', 'grp'))
- residual_gain: float32 [16384], P(('dp', 'grp'))
- chol_rows: float32 [4, 16384], P(None, ('dp', 'grp'))
Inputs may be any that keep to these rules, and one draw needn't show every extreme that they name: Rows 0 to counts - 1 of a device are valid, and one device has 256 valid rows. `dest`: destination device over dp and grp (index over dp+grp); among the valid rows of one device at most 16 name any one destination, and on every device some destination is named by exactly 16 valid rows. `domain_ids`: non-decreasing within each device's rows; a device's rows carry one domain number or two consecutive ones. `winners`: distinct valid rows, on distinct devices.
All inputs are finite; a program needn't handle non-finite values.
Results may differ from a plain program's by a relative error of at most 0.0048.
The roundings to bfloat16 on the way count: a program that leaves them out, or rounds other values in their place, can miss the bound.
Values may be sent and summed in bfloat16 or wider, within the bound.
A program may use at most 64 MiB of HBM per device.

v0:
```python
import jax
import jax.numpy as jnp
from jax import lax
from jax.sharding import PartitionSpec as P

RIDGE = 0.1


def body(embeds, quality, domain_ids, domain_weight, dest, counts, winners):
    shards = lax.axis_size(("dp", "grp"))
    pair_size = lax.axis_size("grp")
    spread_size = lax.axis_size("dp")
    slot_count = embeds.shape[0]
    feature_width = embeds.shape[1]
    step_count = winners.shape[0]
    domains = domain_weight.shape[0]
    per_pair = 2 * slot_count // shards
    balanced = shards * per_pair
    source = lax.axis_index(("dp", "grp"))
    row_index = jnp.arange(slot_count, dtype=jnp.int32)
    is_valid = row_index < counts[0]
    matches = domain_ids[:, None] == jnp.arange(domains, dtype=jnp.int32)[None, :]
    weight_row = jnp.sum(jnp.where(matches, domain_weight[None, :], 0.0), axis=1)
    row_quality = jnp.where(is_valid, quality * weight_row, 0.0).astype(jnp.bfloat16)
    targets = jnp.arange(shards, dtype=jnp.int32)
    dest_hot = ((dest[:, None] == targets[None, :]) & is_valid[:, None]).astype(jnp.bfloat16)
    strictly_lower = (row_index[None, :] < row_index[:, None]).astype(jnp.bfloat16)
    earlier_count = jnp.dot(strictly_lower, dest_hot, preferred_element_type=jnp.float32)
    dest_rank = jnp.sum(jnp.where(dest_hot > 0, earlier_count, 0.0), axis=1).astype(jnp.int32)
    send_slot = jnp.where(is_valid, dest * per_pair + dest_rank, balanced)
    bal_place = (dest * balanced + source * per_pair + dest_rank).astype(jnp.float32)
    send_rows = (
        jnp.zeros((balanced, feature_width), jnp.bfloat16).at[send_slot].set(embeds, mode="drop")
    )
    send_rows = send_rows.reshape(spread_size, pair_size, per_pair, feature_width)
    send_quality = jnp.zeros((balanced,), jnp.bfloat16).at[send_slot].set(row_quality, mode="drop")
    send_quality = send_quality.reshape(spread_size, pair_size, per_pair)
    quality_wide = row_quality.astype(jnp.float32)
    first_hop = (
        lax.all_to_all(send_rows, "dp", split_axis=0, concat_axis=0, tiled=True),
        lax.all_to_all(send_quality, "dp", split_axis=0, concat_axis=0, tiled=True),
    )
    rows_in = lax.all_to_all(first_hop[0], "grp", split_axis=1, concat_axis=1, tiled=True)
    quality_in = lax.all_to_all(first_hop[1], "grp", split_axis=1, concat_axis=1, tiled=True)
    row_norms = jnp.einsum("abmd,abmd->abm", rows_in, rows_in, preferred_element_type=jnp.float32)
    relaid = rows_in.reshape(balanced, feature_width)
    bal_quality = quality_in.reshape(balanced).astype(jnp.float32)
    row_norms = row_norms.reshape(balanced)
    residual_gain = jnp.where(
        bal_quality > 0, bal_quality * bal_quality * row_norms / feature_width + RIDGE, 0.0
    )
    local_place = (source * balanced + jnp.arange(balanced, dtype=jnp.int32)).astype(jnp.float32)
    kept_rows = []
    kept_quality = []
    kept_columns = []
    kept_roots = []
    chol_list = []
    for turn_index in range(step_count):
        chosen = (
            row_index[None, :]
            == (winners[turn_index : turn_index + 1] - source * slot_count)[:, None]
        )
        picked_rows = jnp.dot(
            chosen.astype(jnp.bfloat16), embeds, preferred_element_type=jnp.float32
        )
        picked_quality = jnp.sum(jnp.where(chosen, quality_wide[None, :], 0.0), axis=1)
        picked_place = jnp.sum(jnp.where(chosen, bal_place[None, :], 0.0), axis=1)
        row_sum, quality_sum, place_sum = lax.psum(
            (picked_rows, picked_quality, picked_place), ("dp", "grp")
        )
        row_now = row_sum[0].astype(jnp.bfloat16)
        quality_now = quality_sum[0]
        place_now = place_sum[0]
        dot_now = jnp.dot(relaid, row_now, preferred_element_type=jnp.float32)
        column_now = []
        for prior_step in range(turn_index):
            cross_term = (
                kept_quality[prior_step]
                * quality_now
                * jnp.dot(kept_rows[prior_step], row_now, preferred_element_type=jnp.float32)
                / feature_width
            )
            for earlier in range(prior_step):
                cross_term = cross_term - kept_columns[prior_step][earlier] * column_now[earlier]
            column_now.append(cross_term / kept_roots[prior_step])
        self_term = (
            quality_now
            * quality_now
            * jnp.dot(row_now, row_now, preferred_element_type=jnp.float32)
            / feature_width
            + RIDGE
        )
        for prior_step in range(turn_index):
            self_term = self_term - column_now[prior_step] * column_now[prior_step]
        root_now = jnp.sqrt(self_term)
        inner_sum = jnp.zeros_like(residual_gain)
        for prior_step in range(turn_index):
            inner_sum = inner_sum + chol_list[prior_step] * column_now[prior_step]
        ridge_hit = jnp.where(local_place == place_now, RIDGE, 0.0)
        new_entry = (
            bal_quality * quality_now * dot_now / feature_width + ridge_hit - inner_sum
        ) / root_now
        chol_list.append(new_entry)
        residual_gain = residual_gain - new_entry * new_entry
        kept_rows.append(row_now)
        kept_quality.append(quality_now)
        kept_columns.append(column_now)
        kept_roots.append(root_now)
    return (relaid, residual_gain, jnp.stack(chol_list))


def solution(mesh):
    return jax.shard_map(
        body,
        mesh=mesh,
        in_specs=(
            P(("dp", "grp"), None),
            P(("dp", "grp")),
            P(("dp", "grp")),
            P(),
            P(("dp", "grp")),
            P(("dp", "grp")),
            P(),
        ),
        out_specs=(P(("dp", "grp"), None), P(("dp", "grp")), P(None, ("dp", "grp"))),
        check_vma=False,
    )
```

profile of v0, /device:TPU:0, one launch (start us, length us, event | category | flops | bytes accessed | tf_op | source)
XLA Modules:
  0.0 117.8 jit_solution(18010897146661138979)
XLA Ops:
  0.6 1.4 %fusion.41 = (s32[1]{0:T(128)}, s32[1]{0:T(128)}, s32[1]{0:T(128)}, s32[1]{0:T(128)}) fusion(s32[4]{0:T(128)} %param.13), kind=kLoop, calls=%fused_computation.95 | loop fusion | bytes 32 | tf_op jit(solution)/shard_map/slice | solution.py:61
  5.2 1.0 fusion.1
  6.2 0.8 select_reduce_fusion
  6.9 0.7 add_add_fusion
  7.6 1.4 %fusion.38 = (f32[]{:T(128)}, f32[]{:T(128)}, f32[]{:T(128)}, f32[]{:T(128)}, bf16[256]{0:T(256)(128)(2,1)S(1)}) fusion(s32[]{:T(128)} %bitcast.13, s32[]{:T(128)} %bitcast.7, s32[]{:T(128)} %bitcast.10, s32[]{:T(128)} %bitcast.4, f32[256]{0:T(256)} %param.8, f32[256]{0:T(256)S(1)} %select_reduce_fusion, s32[]{:T(128)} %bitcast.50), kind=kLoop, calls=%fused_computation.81 | loop fusion | flops 4348 | bytes 2596 | tf_op jit(solution)/shard_map/reduce_sum | solution.py:66
  9.0 2.2 %scatter_custom_fusion.1 = bf16[512]{0:T(512)(128)(2,1)S(1)} fusion(s32[256]{0:T(256)S(1)} %get-tuple-element.45, bf16[256]{0:T(256)(128)(2,1)S(1)} %get-tuple-element.38, bf16[]{:T(256)} %constant.18.clone.1), kind=kCustom, calls=%fused_computation.93 | custom fusion | bytes 1026 | tf_op jit(solution)/shard_map/scatter | solution.py:36
  11.2 0.7 reshape.113
  11.9 8.3 %all-to-all-start.2 = ((bf16[16,2,16]{2,1,0:T(2,128)(2,1)}), bf16[16,2,16]{2,1,0:T(2,128)(2,1)S(1)}, u32[]{:S(2)}, u32[]{:S(2)}) async-start(bf16[16,2,16]{2,1,0:T(2,128)(2,1)} %reshape.113), calls=%async_computation.2 | async-start | bytes 16384 | tf_op jit(solution)/shard_map/all_to_all | solution.py:41
  20.2 3.1 %scatter_custom_fusion = bf16[512,1024]{1,0:T(8,128)(2,1)} fusion(s32[256]{0:T(256)S(1)} %get-tuple-element.45, bf16[256,1024]{1,0:T(8,128)(2,1)} %param.7, bf16[]{:T(256)} %constant.18.clone.1), kind=kCustom, calls=%fused_computation.6 | custom fusion | bytes 1049088 | tf_op jit(solution)/shard_map/scatter | solution.py:33
  23.3 4.1 %all-to-all-done.2 = bf16[16,2,16]{2,1,0:T(2,128)(2,1)S(1)} async-done(((bf16[16,2,16]{2,1,0:T(2,128)(2,1)}), bf16[16,2,16]{2,1,0:T(2,128)(2,1)S(1)}, u32[]{:S(2)}, u32[]{:S(2)}) %all-to-all-start.2) | async-done | bytes 1056 | tf_op jit(solution)/shard_map/all_to_all | solution.py:41
  27.4 0.1 reshape.204
  27.5 3.7 %all_to_all.20 = bf16[2,2,128]{2,1,0:T(2,128)(2,1)S(1)} all-to-all(bf16[2,2,128]{2,1,0:T(2,128)(2,1)S(1)} %reshape.204), channel_id=1, replica_groups=mesh['dp'=16,'grp'=2] {'grp'}, dimensions={0} | all-to-all | bytes 2048 | tf_op jit(solution)/shard_map/all_to_all | solution.py:44
  31.2 0.0 copy-start.1
  31.2 3.8 %all-to-all-start = ((bf16[16,2,16,1024]{3,2,1,0:T(8,128)(2,1)}), bf16[16,2,16,1024]{3,2,1,0:T(8,128)(2,1)S(1)}, u32[]{:S(2)}, u32[]{:S(2)}) async-start(bf16[16,2,16,1024]{3,2,1,0:T(8,128)(2,1)} %bitcast.1), calls=%async_computation | async-start | bytes 2097152 | tf_op jit(solution)/shard_map/all_to_all | solution.py:40
  35.1 0.7 select_reduce_fusion.1
  35.8 0.0 copy-done.1
  35.8 0.2 fusion.42
  36.0 0.2 fusion.43
  36.1 0.2 fusion.44
  36.3 0.2 fusion.45
  36.5 47.5 %all-reduce = (f32[]{:T(128)}, bf16[1,1024]{1,0:T(2,128)(2,1)S(1)}, bf16[1,1024]{1,0:T(2,128)(2,1)S(1)}, bf16[1,1024]{1,0:T(2,128)(2,1)S(1)}, bf16[1,1024]{1,0:T...) all-reduce(f32[]{:T(128)} %get-tuple-element.20, ...), channel_id=1, replica_groups=mesh['dp'=16,'grp'=2] {'dp','grp'}, use_global_device_ids=true, to_apply=%region_5.6 | all-reduce | flops 4104 | bytes 24640 | tf_op jit(solution)/shard_map/psum | solution.py:68
  91.9 0.7 fusion.17
  104.4 0.1 reshape.205
  104.5 0.0 all-to-all-done
  104.5 0.1 copy.27
  104.6 4.6 %all_to_all.21 = bf16[16,2,16,1024]{3,2,0,1:T(8,128)(2,1)S(1)} all-to-all(bf16[16,2,16,1024]{3,2,0,1:T(8,128)(2,1)S(1)} %copy.27), channel_id=1, replica_groups=mesh['dp'=16,'grp'=2] {'grp'}, dimensions={1} | all-to-all | bytes 2097152 | tf_op jit(solution)/shard_map/all_to_all | solution.py:43
  109.1 0.1 copy.28
  109.3 0.0 copy-start
  109.3 0.4 fusion.29
  109.6 0.4 fusion.27
  110.0 0.4 fusion.25
  110.4 0.0 copy-done
  110.4 0.4 fusion.23
  110.8 0.3 fusion
  111.1 2.6 %convert_multiply_fusion.4 = (f32[16,2,16]{2,0,1:T(8,128)S(1)}, f32[16,2,16]{2,0,1:T(8,128)S(1)}, f32[16,2,16]{2,0,1:T(8,128)S(1)}, f32[16,2,16]{2,0,1:T(8,128)S(1)}, f32[16,2,16]{2,0,1:T(8,128)S(1)}) fusion(f32[]{:T(128)} %get-tuple-element.21, f32[]{:T(128)} %get-tuple-element.27, f32[]{:T(128)} %get-tuple-element.29, f32[]{:T(128)} %get-tuple-element.31, ...), kind=kLoop, calls=%fused_computation.12 | loop fusion | flops 5632 | bytes 13328 | tf_op jit(solution)/shard_map/mul | solution.py:101
  113.7 0.1 mul.230
  113.8 0.1 mul.240
  113.9 0.1 mul.252
  114.0 0.1 mul.270
  114.1 0.1 reshape.125
  114.2 3.0 %multiply_subtract_fusion = (f32[512]{0:T(512)}, f32[512]{0:T(512)S(1)}, f32[512]{0:T(512)S(1)}, f32[512]{0:T(512)S(1)}, f32[512]{0:T(512)S(1)}) fusion(f32[512]{0:T(512)S(1)} %reshape.125, f32[]{:T(128)S(6)} %sqrt.15, f32[]{:T(128)S(6)} %div.115, f32[]{:T(128)S(6)} %div.113, f32[]{:T(128)S(6)} %div.111, f32[]{:T(128)} %get-tuple-element.32, s32[]{:T(128)S(6)} %mul.232, ...), kind=kLoop, calls=%fused_computation.64 | loop fusion | flops 23552 | bytes 28732 | tf_op jit(solution)/shard_map/sub | solution.py:104
  117.2 0.6 pad_maximum_fusion
  (17 shorter events, 0.2 us)
Async XLA Ops:
  11.9 15.6 %all-to-all-start.2 = ((bf16[16,2,16]{2,1,0:T(2,128)(2,1)}), bf16[16,2,16]{2,1,0:T(2,128)(2,1)S(1)}, u32[]{:S(2)}, u32[]{:S(2)}) async-start(bf16[16,2,16]{2,1,0:T(2,128)(2,1)} %reshape.113), calls=%async_computation.2 | async-start | bytes 16384 | tf_op jit(solution)/shard_map/all_to_all | solution.py:41
  31.2 4.6 %copy-start.1 = (bf16[256,1024]{1,0:T(8,128)(2,1)S(1)}, bf16[256,1024]{1,0:T(8,128)(2,1)}, u32[]{:S(2)}) copy-start(bf16[256,1024]{1,0:T(8,128)(2,1)} %param.7) | copy-start | bytes 1572868
  31.2 73.2 %all-to-all-start = ((bf16[16,2,16,1024]{3,2,1,0:T(8,128)(2,1)}), bf16[16,2,16,1024]{3,2,1,0:T(8,128)(2,1)S(1)}, u32[]{:S(2)}, u32[]{:S(2)}) async-start(bf16[16,2,16,1024]{3,2,1,0:T(8,128)(2,1)} %bitcast.1), calls=%async_computation | async-start | bytes 2097152 | tf_op jit(solution)/shard_map/all_to_all | solution.py:40
  109.3 1.2 copy-start
where the time goes:
time: 119 us; the launch traced here: 118 us
  blocking collectives  55.7 us (47%)
  between operations  23.6 us (20%)
  starting transfers between devices  12.1 us (10%)
  other arithmetic  10.7 us (9%)
  local copies, waits for them, and re-layouts  8.38 us (7%)
  waiting for transfers between devices  4.08 us (3%)
  matrix products  3.22 us (3%)
    psum x1, blocking collectives, body(): lax.psum((picked_rows, picked_quality, picked_place), ('dp', 'grp'))  47.5 us
    all_to_all x1, starting transfers between devices, body(): lax.all_to_all(send_quality, 'dp', split_axis=0, concat_axis=0, tiled=True)  8.34 us
    all_to_all x1, blocking collectives, body(): lax.all_to_all(first_hop[0], 'grp', split_axis=1, concat_axis=1, tiled=True)  4.58 us
    all_to_all x1, waiting for transfers between devices, body(): lax.all_to_all(send_quality, 'dp', split_axis=0, concat_axis=0, tiled=True)  4.08 us
    all_to_all x1, starting transfers between devices, body(): lax.all_to_all(send_rows, 'dp', split_axis=0, concat_axis=0, tiled=True)  3.79 us
    all_to_all x1, blocking collectives, body(): lax.all_to_all(first_hop[1], 'grp', split_axis=1, concat_axis=1, tiled=True)  3.69 us
    scatter x1, local copies, waits for them, and re-layouts, body(): jnp.zeros((balanced, feature_width), jnp.bfloat16).at[send_slot]  3.15 us
    sub x1, other arithmetic, body(): residual_gain = residual_gain - new_entry * new_entry  2.97 us
  transfers between devices with their start and end apart: 2, of which 1 were waited for; matrix products, arithmetic and copies ran while one was open for 5% of the time, Pallas kernels for 0%

commit v1 on v0

v1 whole, which is shorter than its diff:
```python
import functools
import jax
import jax.numpy as jnp
from jax import lax
from jax.experimental import pallas as pl
from jax.experimental.pallas import tpu as pltpu
from jax.sharding import PartitionSpec as P

RIDGE = 0.1
LANES = 128
MESH = pl.DeviceIdType.MESH


def flip(value, bits):
    out = 0
    weight = 1
    while weight <= bits:
        digit = (value // weight) % 2
        out = out + weight * ((1 - digit) if (bits // weight) % 2 else digit)
        weight *= 2
    return out + weight * (value // weight)


def kernel(
    sizes,
    embeds_hbm,
    quality_ref,
    domain_ref,
    dest_ref,
    weight_ref,
    counts_ref,
    winners_ref,
    relaid_hbm,
    gain_ref,
    chol_ref,
    embeds,
    send,
    recv,
    send_quality,
    recv_quality,
    send_winner,
    recv_winner,
    load_sem,
    send_sem,
    recv_sem,
    quality_sem,
    winner_sem,
    store_sem,
):
    pair_size, shards, slots, width, steps, domains = sizes
    per_pair = 2 * slots // shards
    balanced = shards * per_pair
    group = LANES // per_pair
    groups = shards // group
    me_dp = lax.axis_index("dp")
    me_grp = lax.axis_index("grp")
    me = me_dp * pair_size + me_grp
    my_group = me // group
    my_local = me % group

    load = pltpu.make_async_copy(embeds_hbm, embeds, load_sem)
    load.start()
    barrier = pltpu.get_barrier_semaphore()

    @pl.loop(1, shards)
    def _(k):
        peer = (me + k) % shards
        pl.semaphore_signal(
            barrier,
            inc=1,
            device_id=(peer // pair_size, peer % pair_size),
            device_id_type=MESH,
        )

    dest = dest_ref[...]
    row = lax.broadcasted_iota(jnp.int32, (1, slots), 1)
    valid = row < counts_ref[0]
    domain = domain_ref[...]
    weight = jnp.zeros((1, slots), jnp.float32)
    for d in range(domains):
        weight = jnp.where(domain == d, weight_ref[d], weight)
    quality = jnp.where(valid, quality_ref[...] * weight, 0.0)
    quality = quality.astype(jnp.bfloat16).astype(jnp.float32)
    target = lax.broadcasted_iota(jnp.int32, (shards, slots), 0)
    hot = (target == dest) & valid
    hot_wide = jnp.where(hot, 1.0, 0.0)
    before = jnp.where(
        lax.broadcasted_iota(jnp.int32, (slots, slots), 0)
        < lax.broadcasted_iota(jnp.int32, (slots, slots), 1),
        1.0,
        0.0,
    ).astype(jnp.bfloat16)
    earlier = jnp.dot(
        hot_wide.astype(jnp.bfloat16), before, preferred_element_type=jnp.float32
    )
    rank = jnp.sum(jnp.where(hot, earlier, 0.0), axis=0, keepdims=True)
    rank = rank.astype(jnp.int32)
    slot = jnp.where(valid, dest * per_pair + rank, -1)
    place = (dest * balanced + me * per_pair + rank).astype(jnp.float32)

    lane_rank = lax.broadcasted_iota(jnp.int32, (LANES, slots), 0)
    rank_hot = jnp.where(lane_rank == rank + my_local * per_pair, 1.0, 0.0)
    spread = lax.dot_general(
        jnp.where(hot, quality, 0.0).astype(jnp.bfloat16),
        rank_hot.astype(jnp.bfloat16),
        (((1,), (1,)), ((), ())),
        preferred_element_type=jnp.float32,
    )
    send_quality[...] = spread.reshape(shards, 1, LANES)

    chosen = row < 0
    lane = lax.broadcasted_iota(jnp.int32, (1, LANES), 1)
    meta = jnp.zeros((1, LANES), jnp.float32)
    for t in range(steps):
        local = winners_ref[t] - me * slots
        chosen_now = row == local
        chosen = chosen | chosen_now
        mine = jnp.where((local >= 0) & (local < slots), 1.0, 0.0)
        meta = jnp.where(lane == t, mine, meta)
    won_quality = jnp.sum(jnp.where(chosen, quality, 0.0), axis=1, keepdims=True)
    won_place = jnp.sum(jnp.where(chosen, place, 0.0), axis=1, keepdims=True)
    meta = jnp.where(lane == steps, won_quality, meta)
    meta = jnp.where(lane == steps + 1, won_place, meta)
    send_winner[:, width:] = meta
    load.wait()
    picked = jnp.dot(
        jnp.broadcast_to(jnp.where(chosen, 1.0, 0.0), (16, slots)).astype(jnp.bfloat16),
        embeds[...],
        preferred_element_type=jnp.float32,
    )
    send_winner[:, :width] = picked[0:1]

    slot_index = lax.broadcasted_iota(jnp.int32, (balanced, slots), 0)
    permute = jnp.where(slot_index == slot, 1.0, 0.0).astype(jnp.bfloat16)
    for c in range(0, width, 256):
        moved = jnp.dot(
            permute, embeds[:, c : c + 256], preferred_element_type=jnp.float32
        )
        send[:, :, c : c + 256] = moved.astype(jnp.bfloat16).reshape(shards, per_pair, 256)

    own_rows = pltpu.make_async_copy(send.at[me], recv.at[me], recv_sem.at[my_group])
    own_quality = pltpu.make_async_copy(
        send_quality.at[me], recv_quality.at[me], quality_sem.at[my_group]
    )
    own_winner = pltpu.make_async_copy(send_winner, recv_winner.at[me], winner_sem)

    pl.semaphore_wait(barrier, shards - 1)

    def peer_of(bits, k):
        peer = flip(my_group, bits) * group + (my_local + k) % group
        return peer, (peer // pair_size, peer % pair_size)

    def over_peers(fn):
        for bits in range(groups - 1, -1, -1):

            @pl.loop(0 if bits else 1, group)
            def _(k):
                fn(*peer_of(bits, k))

    def send_small(peer, device):
        pltpu.make_async_remote_copy(
            src_ref=send_winner,
            dst_ref=recv_winner.at[me],
            send_sem=send_sem.at[0],
            recv_sem=winner_sem,
            device_id=device,
            device_id_type=MESH,
        ).start()

    def send_rows(peer, device):
        pltpu.make_async_remote_copy(
            src_ref=send_quality.at[peer],
            dst_ref=recv_quality.at[me],
            send_sem=send_sem.at[1],
            recv_sem=quality_sem.at[my_group],
            device_id=device,
            device_id_type=MESH,
        ).start()
        pltpu.make_async_remote_copy(
            src_ref=send.at[peer],
            dst_ref=recv.at[me],
            send_sem=send_sem.at[2],
            recv_sem=recv_sem.at[my_group],
            device_id=device,
            device_id_type=MESH,
        ).start()

    over_peers(send_small)
    own_winner.start()
    over_peers(send_rows)
    own_rows.start()
    own_quality.start()

    pltpu.make_async_copy(recv_winner, recv_winner, winner_sem).wait()
    heard = recv_winner[...].reshape(shards, width + LANES)
    kept = []
    for t in range(steps):
        pick = heard[:, width + t : width + t + 1]
        kept.append(jnp.sum(heard * pick, axis=0, keepdims=True))
    step_row = lax.broadcasted_iota(jnp.int32, (16, width), 0)
    wins = jnp.zeros((16, width), jnp.float32)
    for t in range(steps):
        wins = jnp.where(step_row == t, kept[t][:, :width], wins)
    wins = wins.astype(jnp.bfloat16)
    gram = lax.dot_general(
        wins, wins, (((1,), (1,)), ((), ())), preferred_element_type=jnp.float32
    )
    win_quality = [kept[t][:, width + steps : width + steps + 1] for t in range(steps)]
    win_place = [kept[t][:, width + steps + 1 : width + steps + 2] for t in range(steps)]
    columns = []
    roots = []
    for t in range(steps):
        column = []
        for k in range(t):
            cross = win_quality[k] * win_quality[t] * gram[k : k + 1, t : t + 1] / width
            for e in range(k):
                cross = cross - columns[k][e] * column[e]
            column.append(cross / roots[k])
        left = win_quality[t] * win_quality[t] * gram[t : t + 1, t : t + 1] / width + RIDGE
        for k in range(t):
            left = left - column[k] * column[k]
        columns.append(column)
        roots.append(jnp.sqrt(left))

    for bits in range(groups):
        here = flip(my_group, bits)
        first = here * group
        blocks = recv.at[pl.ds(first, group)]
        scores = recv_quality.at[pl.ds(first, group)]
        pltpu.make_async_copy(blocks, blocks, recv_sem.at[here]).wait()
        pltpu.make_async_copy(scores, scores, quality_sem.at[here]).wait()
        pltpu.make_async_copy(
            blocks, relaid_hbm.at[pl.ds(first, group)], store_sem.at[bits]
        ).start()
        rows = blocks[...].reshape(LANES, width)
        bal_quality = jnp.sum(scores[...].reshape(group, LANES), axis=0, keepdims=True)
        dots = lax.dot_general(
            wins, rows, (((1,), (1,)), ((), ())), preferred_element_type=jnp.float32
        )
        total = jnp.zeros((LANES, LANES), jnp.float32)
        for c in range(0, width, LANES):
            part = rows[:, c : c + LANES].astype(jnp.float32)
            total = total + part * part
        norms = jnp.sum(total.T, axis=0, keepdims=True)
        gain = jnp.where(
            bal_quality > 0, bal_quality * bal_quality * norms / width + RIDGE, 0.0
        )
        at = (me * balanced + here * LANES + lane).astype(jnp.float32)
        span = pl.ds(pl.multiple_of(here * LANES, LANES), LANES)
        entries = []
        for t in range(steps):
            inner = jnp.zeros((1, LANES), jnp.float32)
            for k in range(t):
                inner = inner + entries[k] * columns[t][k]
            hit = jnp.where(at == win_place[t], RIDGE, 0.0)
            entry = (
                bal_quality * win_quality[t] * dots[t : t + 1] / width + hit - inner
            ) / roots[t]
            entries.append(entry)
            gain = gain - entry * entry
            chol_ref[t : t + 1, span] = entry
        gain_ref[:, span] = gain

    for bits in range(groups):
        blocks = recv.at[pl.ds(flip(my_group, bits) * group, group)]
        pltpu.make_async_copy(
            blocks, relaid_hbm.at[pl.ds(flip(my_group, bits) * group, group)], store_sem.at[bits]
        ).wait()
    others = recv_winner.at[pl.ds(0, shards - 1)]
    pltpu.make_async_copy(others, others, send_sem.at[0]).wait()
    others = send_quality.at[pl.ds(0, shards - 1)]
    pltpu.make_async_copy(others, others, send_sem.at[1]).wait()
    others = send.at[pl.ds(0, shards - 1)]
    pltpu.make_async_copy(others, others, send_sem.at[2]).wait()


def body(embeds, quality, domain_ids, domain_weight, dest, counts, winners):
    shards = lax.axis_size(("dp", "grp"))
    pair_size = lax.axis_size("grp")
    slots, width = embeds.shape
    steps = winners.shape[0]
    domains = domain_weight.shape[0]
    per_pair = 2 * slots // shards
    balanced = shards * per_pair
    groups = balanced // LANES
    vmem = pl.BlockSpec(memory_space=pltpu.VMEM)
    smem = pl.BlockSpec(memory_space=pltpu.SMEM)
    anywhere = pl.BlockSpec(memory_space=pl.ANY)
    dma = pltpu.SemaphoreType.DMA
    relaid, gain, chol = pl.pallas_call(
        functools.partial(kernel, (pair_size, shards, slots, width, steps, domains)),
        out_shape=(
            jax.ShapeDtypeStruct((shards, per_pair, width), jnp.bfloat16),
            jax.ShapeDtypeStruct((1, balanced), jnp.float32),
            jax.ShapeDtypeStruct((steps, balanced), jnp.float32),
        ),
        in_specs=[anywhere, vmem, vmem, vmem, smem, smem, smem],
        out_specs=(anywhere, vmem, vmem),
        scratch_shapes=[
            pltpu.VMEM((slots, width), jnp.bfloat16),
            pltpu.VMEM((shards, per_pair, width), jnp.bfloat16),
            pltpu.VMEM((shards, per_pair, width), jnp.bfloat16),
            pltpu.VMEM((shards, 1, LANES), jnp.float32),
            pltpu.VMEM((shards, 1, LANES), jnp.float32),
            pltpu.VMEM((1, width + LANES), jnp.float32),
            pltpu.VMEM((shards, 1, width + LANES), jnp.float32),
            dma,
            dma((3,)),
            dma((groups,)),
            dma((groups,)),
            dma,
            dma((groups,)),
        ],
        compiler_params=pltpu.CompilerParams(collective_id=0, has_side_effects=True),
        name="relay_select",
    )(
        embeds,
        quality.reshape(1, slots),
        domain_ids.reshape(1, slots),
        dest.reshape(1, slots),
        domain_weight,
        counts,
        winners,
    )
    return relaid.reshape(balanced, width), gain.reshape(balanced), chol


def solution(mesh):
    return jax.shard_map(
        body,
        mesh=mesh,
        in_specs=(
            P(("dp", "grp"), None),
            P(("dp", "grp")),
            P(("dp", "grp")),
            P(),
            P(("dp", "grp")),
            P(("dp", "grp")),
            P(),
        ),
        out_specs=(P(("dp", "grp"), None), P(("dp", "grp")), P(None, ("dp", "grp"))),
        check_vma=False,
    )
```

time: 119 us -> 42.3 us (0.36)
  blocking collectives: 55.7 us -> 0 us
  Pallas kernels: 0 us -> 37.4 us
  between operations: 23.6 us -> 1.3 us
  starting transfers between devices: 12.1 us -> 0 us
  other arithmetic: 10.7 us -> 0 us
  local copies, waits for them, and re-layouts: 8.38 us -> 3.45 us
  waiting for transfers between devices: 4.08 us -> 0 us
  matrix products: 3.22 us -> 0 us
    psum x1 -> x0, blocking collectives: 47.5 us -> none  [body(): lax.psum((picked_rows, picked_quality, picked_place), ('dp', 'grp'))]
    pallas_call x0 -> x1, Pallas kernels: none -> 37.4 us  [body(): pl.pallas_call(functools.partial(kernel, (pair_size, shards, slots, width...]
    all_to_all x2 -> x0, starting transfers between devices: 12.1 us -> none  [the longest x1 8.34 us: body(): lax.all_to_all(send_quality, 'dp', split_axis=0, concat_axis=0, tiled=True)]
    all_to_all x2 -> x0, blocking collectives: 8.26 us -> none  [the longest x1 4.58 us: body(): lax.all_to_all(first_hop[0], 'grp', split_axis=1, concat_axis=1, tiled=True)]
    scatter x2 -> x0, local copies, waits for them, and re-layouts: 5.3 us -> none  [the longest x1 3.15 us: body(): jnp.zeros((balanced, feature_width), jnp.bfloat16).at[send_slot]]
    all_to_all x2 -> x0, waiting for transfers between devices: 4.08 us -> none  [the longest x1 4.08 us: body(): lax.all_to_all(send_quality, 'dp', split_axis=0, concat_axis=0, tiled=True)]
    unnamed x6 -> x7, local copies, waits for them, and re-layouts: 0.19 us -> 3.45 us
    dot_general x9 -> x0, matrix products: 3.22 us -> none  [the longest x4 1.53 us: body(): dot_now = jnp.dot(relaid, row_now, preferred_element_type=jnp.float32)]
  transfers between devices with their start and end apart: 2 -> 0, of which waited for: 1 -> 0; matrix products, arithmetic and copies ran while one was open for 5% -> 0% of each run, Pallas kernels for 0% -> 0%
where the time goes in v1:
time: 42.3 us; the launch traced here: 42.1 us
  Pallas kernels  37.4 us (88%)
  local copies, waits for them, and re-layouts  3.45 us (8%)
  between operations  1.3 us (3%)
    pallas_call x1, Pallas kernels, body(): pl.pallas_call(functools.partial(kernel, (pair_size, shards, slots, width...  37.4 us
    unnamed x7, local copies, waits for them, and re-layouts  3.45 us

profile of v1, /device:TPU:0, one launch (start us, length us, event | category | flops | bytes accessed | tf_op | source)
XLA Modules:
  0.0 42.1 jit_solution(17357690330778233751)
XLA Ops:
  1.3 37.4 %relay_select.1 = (bf16[32,16,1024]{2,1,0:T(8,128)(2,1)}, f32[1,512]{1,0:T(1,128)}, f32[4,512]{1,0:T(4,128)}) custom-call(bf16[256,1024]{1,0:T(8,128)(2,1)} %embeds_hbm.1, f32[1,256]{1,0:T(1,128)} %bitcast.7, s32[1,256]{1,0:T(1,128)} %bitcast.8, s32[1,256]{1,0:T(1,128)} %bitcast.9, f32[16]{0:T(128)} %weight_ref.1, s32[1]{0:T(128)S(6)} %copy.13.counts_ref, ...), custom_call_target="tpu_custom_call" | custom-call | tf_op jit(solution)/shard_map/relay_select/pallas_call | solution.py:290
  38.6 0.0 copy-start.1
  38.7 0.0 copy-start
  38.7 2.3 %copy.14 = bf16[512,1024]{1,0:T(8,128)(2,1)} copy(bf16[512,1024]{1,0:T(8,128)(2,1)} %bitcast.5) | data formatting | bytes 2097152
  40.9 0.0 copy-done.1
  40.9 0.6 %copy.15 = f32[512]{0:T(512)} copy(f32[512]{0:T(512)S(1)} %bitcast.6) | data formatting | bytes 4096
  41.5 0.0 copy-done
  41.5 0.6 %copy.16 = f32[4,512]{1,0:T(4,128)} copy(f32[4,512]{1,0:T(4,128)S(1)} %copy-done) | data formatting | bytes 16384
Async XLA Ops:
  38.6 2.3 %copy-start.1 = (f32[1,512]{1,0:T(1,128)S(1)}, f32[1,512]{1,0:T(1,128)}, u32[]{:S(2)}) copy-start(f32[1,512]{1,0:T(1,128)} %get-tuple-element.7) | copy-start | bytes 6148
  38.7 2.9 %copy-start = (f32[4,512]{1,0:T(4,128)S(1)}, f32[4,512]{1,0:T(4,128)}, u32[]{:S(2)}) copy-start(f32[4,512]{1,0:T(4,128)} %get-tuple-element.14) | copy-start | bytes 24580

commit v2 on v1

--- a/solution.py
+++ b/solution.py
@@ -30,12 +30,10 @@
     weight_ref,
     counts_ref,
     winners_ref,
-    relaid_hbm,
-    gain_ref,
-    chol_ref,
+    recv,
+    result_ref,
     embeds,
     send,
-    recv,
     send_quality,
     recv_quality,
     send_winner,
@@ -45,11 +43,12 @@
     recv_sem,
     quality_sem,
     winner_sem,
-    store_sem,
+    mate_sem,
 ):
     pair_size, shards, slots, width, steps, domains = sizes
     per_pair = 2 * slots // shards
     balanced = shards * per_pair
+    spread_size = shards // pair_size
     group = LANES // per_pair
     groups = shards // group
     me_dp = lax.axis_index("dp")
@@ -106,29 +105,36 @@
         (((1,), (1,)), ((), ())),
         preferred_element_type=jnp.float32,
     )
-    send_quality[...] = spread.reshape(shards, 1, LANES)
 
     chosen = row < 0
     lane = lax.broadcasted_iota(jnp.int32, (1, LANES), 1)
+    lane_fact = (lane + (LANES - (my_local + 1) * per_pair)) % LANES
     meta = jnp.zeros((1, LANES), jnp.float32)
     for t in range(steps):
         local = winners_ref[t] - me * slots
         chosen_now = row == local
         chosen = chosen | chosen_now
         mine = jnp.where((local >= 0) & (local < slots), 1.0, 0.0)
-        meta = jnp.where(lane == t, mine, meta)
+        meta = jnp.where(lane_fact == t, mine, meta)
     won_quality = jnp.sum(jnp.where(chosen, quality, 0.0), axis=1, keepdims=True)
     won_place = jnp.sum(jnp.where(chosen, place, 0.0), axis=1, keepdims=True)
-    meta = jnp.where(lane == steps, won_quality, meta)
-    meta = jnp.where(lane == steps + 1, won_place, meta)
-    send_winner[:, width:] = meta
+    meta = jnp.where(lane_fact == steps, won_quality, meta)
+    meta = jnp.where(lane_fact == steps + 1, won_place, meta)
+    send_quality[...] = (spread + meta).reshape(shards, 1, LANES)
     load.wait()
     picked = jnp.dot(
         jnp.broadcast_to(jnp.where(chosen, 1.0, 0.0), (16, slots)).astype(jnp.bfloat16),
         embeds[...],
         preferred_element_type=jnp.float32,
     )
-    send_winner[:, :width] = picked[0:1]
+    folds = width // LANES
+    fold_row = lax.broadcasted_iota(jnp.int32, (folds, LANES), 0)
+    folded = jnp.zeros((folds, LANES), jnp.float32)
+    for f in range(folds):
+        folded = jnp.where(
+            fold_row == f, picked[0:1, f * LANES : (f + 1) * LANES], folded
+        )
+    send_winner[...] = folded.astype(jnp.bfloat16)
 
     slot_index = lax.broadcasted_iota(jnp.int32, (balanced, slots), 0)
     permute = jnp.where(slot_index == slot, 1.0, 0.0).astype(jnp.bfloat16)
@@ -142,32 +148,28 @@
     own_quality = pltpu.make_async_copy(
         send_quality.at[me], recv_quality.at[me], quality_sem.at[my_group]
     )
-    own_winner = pltpu.make_async_copy(send_winner, recv_winner.at[me], winner_sem)
+    own_winner = pltpu.make_async_copy(
+        send_winner, recv_winner.at[me_grp, me_dp], winner_sem.at[0]
+    )
 
     pl.semaphore_wait(barrier, shards - 1)
 
-    def peer_of(bits, k):
-        peer = flip(my_group, bits) * group + (my_local + k) % group
-        return peer, (peer // pair_size, peer % pair_size)
-
-    def over_peers(fn):
-        for bits in range(groups - 1, -1, -1):
-
-            @pl.loop(0 if bits else 1, group)
-            def _(k):
-                fn(*peer_of(bits, k))
-
-    def send_small(peer, device):
+    @pl.loop(1, spread_size)
+    def _(k):
         pltpu.make_async_remote_copy(
             src_ref=send_winner,
-            dst_ref=recv_winner.at[me],
+            dst_ref=recv_winner.at[me_grp, me_dp],
             send_sem=send_sem.at[0],
-            recv_sem=winner_sem,
-            device_id=device,
+            recv_sem=winner_sem.at[0],
+            device_id=((me_dp + k) % spread_size, me_grp),
             device_id_type=MESH,
         ).start()
 
-    def send_rows(peer, device):
+    own_winner.start()
+
+    def send_rows(bits, k):
+        peer = flip(my_group, bits) * group + (my_local + k) % group
+        device = (peer // pair_size, peer % pair_size)
         pltpu.make_async_remote_copy(
             src_ref=send_quality.at[peer],
             dst_ref=recv_quality.at[me],
@@ -185,28 +187,80 @@
             device_id_type=MESH,
         ).start()
 
-    over_peers(send_small)
-    own_winner.start()
-    over_peers(send_rows)
+    @pl.loop(0, group)
+    def _(k):
+        for bits in range(groups - 1, 0, -1):
+            send_rows(bits, k)
+
+        @pl.when(k > 0)
+        def _():
+            send_rows(0, k)
+
     own_rows.start()
     own_quality.start()
 
-    pltpu.make_async_copy(recv_winner, recv_winner, winner_sem).wait()
-    heard = recv_winner[...].reshape(shards, width + LANES)
-    kept = []
+    mine = recv_winner.at[me_grp]
+    pltpu.make_async_copy(mine, mine, winner_sem.at[0]).wait()
+    relays = []
+    for k in range(1, pair_size):
+        relay = pltpu.make_async_remote_copy(
+            src_ref=mine,
+            dst_ref=mine,
+            send_sem=mate_sem.at[0, k - 1],
+            recv_sem=mate_sem.at[1, k - 1],
+            device_id=(me_dp, (me_grp + k) % pair_size),
+            device_id_type=MESH,
+        )
+        relay.start()
+        relays.append(relay)
+    for relay in relays:
+        relay.wait()
+    for g in range(groups):
+        scores = recv_quality.at[pl.ds(g * group, group)]
+        pltpu.make_async_copy(scores, scores, quality_sem.at[g]).wait()
+
+    facts = recv_quality[...].reshape(shards, LANES)
+    source = lax.broadcasted_iota(jnp.int32, (shards, LANES), 0)
+    fact_lane = lax.broadcasted_iota(jnp.int32, (shards, LANES), 1)
+    fact = (fact_lane + (LANES - (source % group + 1) * per_pair)) % LANES
+    def fact_of(i):
+        return jnp.sum(jnp.where(fact == i, facts, 0.0), axis=1, keepdims=True)
+
+    owners = [fact_of(t) for t in range(steps)]
+    source_quality = fact_of(steps)
+    source_place = fact_of(steps + 1)
+    win_quality = [jnp.sum(o * source_quality, axis=0, keepdims=True) for o in owners]
+    win_place = [jnp.sum(o * source_place, axis=0, keepdims=True) for o in owners]
+    owner_table = jnp.zeros((shards, LANES), jnp.float32)
     for t in range(steps):
-        pick = heard[:, width + t : width + t + 1]
-        kept.append(jnp.sum(heard * pick, axis=0, keepdims=True))
-    step_row = lax.broadcasted_iota(jnp.int32, (16, width), 0)
-    wins = jnp.zeros((16, width), jnp.float32)
-    for t in range(steps):
-        wins = jnp.where(step_row == t, kept[t][:, :width], wins)
-    wins = wins.astype(jnp.bfloat16)
+        owner_table = jnp.where(fact_lane == t, owners[t], owner_table)
+    line = lax.broadcasted_iota(jnp.int32, (shards, shards * folds), 1)
+    order = line // folds
+    line_source = (order % spread_size) * pair_size + order // spread_size
+    line_hot = jnp.where(
+        line_source == lax.broadcasted_iota(jnp.int32, line.shape, 0), 1.0, 0.0
+    )
+    spread_owner = jnp.dot(
+        owner_table.T[:16].astype(jnp.bfloat16),
+        line_hot.astype(jnp.bfloat16),
+        preferred_element_type=jnp.float32,
+    )
+    lines = recv_winner[...].reshape(shards * folds, LANES)
+    line_fold = lax.broadcasted_iota(jnp.int32, spread_owner.shape, 1) % folds
+    wins = jnp.concatenate(
+        [
+            jnp.dot(
+                jnp.where(line_fold == f, spread_owner, 0.0).astype(jnp.bfloat16),
+                lines,
+                preferred_element_type=jnp.float32,
+            )
+            for f in range(folds)
+        ],
+        axis=1,
+    ).astype(jnp.bfloat16)
     gram = lax.dot_general(
         wins, wins, (((1,), (1,)), ((), ())), preferred_element_type=jnp.float32
     )
-    win_quality = [kept[t][:, width + steps : width + steps + 1] for t in range(steps)]
-    win_place = [kept[t][:, width + steps + 1 : width + steps + 2] for t in range(steps)]
     columns = []
     roots = []
     for t in range(steps):
@@ -228,12 +282,14 @@
         blocks = recv.at[pl.ds(first, group)]
         scores = recv_quality.at[pl.ds(first, group)]
         pltpu.make_async_copy(blocks, blocks, recv_sem.at[here]).wait()
-        pltpu.make_async_copy(scores, scores, quality_sem.at[here]).wait()
-        pltpu.make_async_copy(
-            blocks, relaid_hbm.at[pl.ds(first, group)], store_sem.at[bits]
-        ).start()
         rows = blocks[...].reshape(LANES, width)
-        bal_quality = jnp.sum(scores[...].reshape(group, LANES), axis=0, keepdims=True)
+        own_lane = lax.broadcasted_iota(jnp.int32, (group, LANES), 1) // per_pair
+        own_lane = own_lane == lax.broadcasted_iota(jnp.int32, (group, LANES), 0)
+        bal_quality = jnp.sum(
+            jnp.where(own_lane, scores[...].reshape(group, LANES), 0.0),
+            axis=0,
+            keepdims=True,
+        )
         dots = lax.dot_general(
             wins, rows, (((1,), (1,)), ((), ())), preferred_element_type=jnp.float32
         )
@@ -258,20 +314,23 @@
             ) / roots[t]
             entries.append(entry)
             gain = gain - entry * entry
-            chol_ref[t : t + 1, span] = entry
-        gain_ref[:, span] = gain
-
-    for bits in range(groups):
-        blocks = recv.at[pl.ds(flip(my_group, bits) * group, group)]
-        pltpu.make_async_copy(
-            blocks, relaid_hbm.at[pl.ds(flip(my_group, bits) * group, group)], store_sem.at[bits]
-        ).wait()
-    others = recv_winner.at[pl.ds(0, shards - 1)]
+            result_ref[t : t + 1, span] = entry
+        result_ref[steps : steps + 1, span] = gain
+
+    others = recv_winner.at[0, pl.ds(0, spread_size - 1)]
     pltpu.make_async_copy(others, others, send_sem.at[0]).wait()
     others = send_quality.at[pl.ds(0, shards - 1)]
     pltpu.make_async_copy(others, others, send_sem.at[1]).wait()
     others = send.at[pl.ds(0, shards - 1)]
     pltpu.make_async_copy(others, others, send_sem.at[2]).wait()
+
+
+def write_kernel(steps, rows_ref, result_ref, relaid_hbm, gain_ref, chol_ref, sem):
+    copy = pltpu.make_async_copy(rows_ref, relaid_hbm, sem)
+    copy.start()
+    gain_ref[...] = result_ref[steps : steps + 1]
+    chol_ref[...] = result_ref[:steps]
+    copy.wait()
 
 
 def body(embeds, quality, domain_ids, domain_weight, dest, counts, winners):
@@ -285,33 +344,34 @@
     groups = balanced // LANES
     vmem = pl.BlockSpec(memory_space=pltpu.VMEM)
     smem = pl.BlockSpec(memory_space=pltpu.SMEM)
-    anywhere = pl.BlockSpec(memory_space=pl.ANY)
+    hbm = pl.BlockSpec(memory_space=pltpu.HBM)
     dma = pltpu.SemaphoreType.DMA
-    relaid, gain, chol = pl.pallas_call(
+    folds = width // LANES
+    rows, result = pl.pallas_call(
         functools.partial(kernel, (pair_size, shards, slots, width, steps, domains)),
         out_shape=(
-            jax.ShapeDtypeStruct((shards, per_pair, width), jnp.bfloat16),
-            jax.ShapeDtypeStruct((1, balanced), jnp.float32),
-            jax.ShapeDtypeStruct((steps, balanced), jnp.float32),
+            pltpu.VMEM((shards, per_pair, width), jnp.bfloat16),
+            pltpu.VMEM((8, balanced), jnp.float32),
         ),
-        in_specs=[anywhere, vmem, vmem, vmem, smem, smem, smem],
-        out_specs=(anywhere, vmem, vmem),
+        in_specs=[hbm, vmem, vmem, vmem, smem, smem, smem],
+        out_specs=(vmem, vmem),
         scratch_shapes=[
             pltpu.VMEM((slots, width), jnp.bfloat16),
             pltpu.VMEM((shards, per_pair, width), jnp.bfloat16),
-            pltpu.VMEM((shards, per_pair, width), jnp.bfloat16),
             pltpu.VMEM((shards, 1, LANES), jnp.float32),
             pltpu.VMEM((shards, 1, LANES), jnp.float32),
-            pltpu.VMEM((1, width + LANES), jnp.float32),
-            pltpu.VMEM((shards, 1, width + LANES), jnp.float32),
+            pltpu.VMEM((folds, LANES), jnp.bfloat16),
+            pltpu.VMEM((pair_size, shards // pair_size, folds, LANES), jnp.bfloat16),
             dma,
             dma((3,)),
             dma((groups,)),
             dma((groups,)),
-            dma,
-            dma((groups,)),
+            dma((1,)),
+            dma((2, pair_size - 1)),
         ],
-        compiler_params=pltpu.CompilerParams(collective_id=0, has_side_effects=True),
+        compiler_params=pltpu.CompilerParams(
+            collective_id=0, has_side_effects=True, vmem_limit_bytes=24 * 1024 * 1024
+        ),
         name="relay_select",
     )(
         embeds,
@@ -322,6 +382,19 @@
         counts,
         winners,
     )
+    relaid, gain, chol = pl.pallas_call(
+        functools.partial(write_kernel, steps),
+        out_shape=(
+            jax.ShapeDtypeStruct((shards, per_pair, width), jnp.bfloat16),
+            jax.ShapeDtypeStruct((1, balanced), jnp.float32),
+            jax.ShapeDtypeStruct((steps, balanced), jnp.float32),
+        ),
+        in_specs=[vmem, vmem],
+        out_specs=(hbm, vmem, vmem),
+        scratch_shapes=[dma],
+        compiler_params=pltpu.CompilerParams(vmem_limit_bytes=8 * 1024 * 1024),
+        name="write_out",
+    )(rows, result)
     return relaid.reshape(balanced, width), gain.reshape(balanced), chol
 
 

time: 42.3 us -> 39.1 us (0.924)
  local copies, waits for them, and re-layouts: 3.45 us -> 1.73 us
  Pallas kernels: 37.4 us -> 35.8 us
    pallas_call x1, Pallas kernels: 37.4 us -> 34.3 us  [body(): pl.pallas_call(functools.partial(kernel, (pair_size, shards, slots, width...]
    unnamed x7 -> x12, local copies, waits for them, and re-layouts: 3.45 us -> 1.73 us
    pallas_call x0 -> x1, Pallas kernels: none -> 1.58 us  [body(): pl.pallas_call(functools.partial(write_kernel, steps), out_shape=(jax.Sha...]
where the time goes in v2:
time: 39.1 us; the launch traced here: 38.9 us
  Pallas kernels  35.8 us (92%)
  local copies, waits for them, and re-layouts  1.73 us (4%)
  between operations  1.33 us (3%)
    pallas_call x1, Pallas kernels, body(): pl.pallas_call(functools.partial(kernel, (pair_size, shards, slots, width...  34.3 us
    unnamed x12, local copies, waits for them, and re-layouts  1.73 us
    pallas_call x1, Pallas kernels, body(): pl.pallas_call(functools.partial(write_kernel, steps), out_shape=(jax.Sha...  1.58 us

profile of v2, /device:TPU:0, one launch (start us, length us, event | category | flops | bytes accessed | tf_op | source)
XLA Modules:
  0.0 38.9 jit_solution(15288287489540211767)
XLA Ops:
  1.3 0.0 copy-start.5
  1.3 0.0 copy-start.2
  1.3 0.0 copy-start.3
  1.3 0.0 copy-start.1
  1.3 0.0 copy-start.4
  1.3 0.6 %copy-done.5 = s32[4]{0:T(128)S(1)} copy-done((s32[4]{0:T(128)S(1)}, s32[4]{0:T(128)}, u32[]{:S(2)}) %copy-start.5) | copy-done | bytes 40
  1.9 0.0 copy-done.2
  2.0 0.0 copy-done.3
  2.0 0.0 copy-done.1
  2.0 0.0 copy-done.4
  2.0 0.0 copy-start
  2.0 1.0 %copy-done = bf16[256,1024]{1,0:T(8,128)(2,1)S(1)} copy-done((bf16[256,1024]{1,0:T(8,128)(2,1)S(1)}, bf16[256,1024]{1,0:T(8,128)(2,1)}, u32[]{:S(2)}) %copy-start) | copy-done | bytes 524312
  3.1 34.3 %relay_select.1 = (bf16[32,16,1024]{2,1,0:T(8,128)(2,1)S(1)}, f32[8,512]{1,0:T(8,128)S(1)}) custom-call(bf16[256,1024]{1,0:T(8,128)(2,1)S(1)} %copy-done, f32[1,256]{1,0:T(1,128)S(1)} %bitcast.5, s32[1,256]{1,0:T(1,128)S(1)} %bitcast.6, s32[1,256]{1,0:T(1,128)S(1)} %bitcast.7, f32[16]{0:T(128)S(1)} %copy-done.4, s32[1]{0:T(128)S(6)} %copy.10.counts_ref, ...), custom_call_target="tpu_custom_call" | custom-call | tf_op jit(solution)/shard_map/relay_select/pallas_call | solution.py:350
  37.3 1.6 %write_out.1 = (bf16[32,16,1024]{2,1,0:T(8,128)(2,1)}, f32[1,512]{1,0:T(1,128)}, f32[4,512]{1,0:T(4,128)}) custom-call(bf16[32,16,1024]{2,1,0:T(8,128)(2,1)S(1)} %get-tuple-element.8.rows_ref, f32[8,512]{1,0:T(8,128)S(1)} %get-tuple-element.9.result_ref), custom_call_target="tpu_custom_call" | custom-call | tf_op jit(solution)/shard_map/write_out/pallas_call | solution.py:385
Async XLA Ops:
  1.3 0.7 %copy-start.5 = (s32[4]{0:T(128)S(1)}, s32[4]{0:T(128)}, u32[]{:S(2)}) copy-start(s32[4]{0:T(128)} %winners_ref.1) | copy-start | bytes 52
  1.3 0.7 %copy-start.2 = (s32[256]{0:T(256)S(1)}, s32[256]{0:T(256)}, u32[]{:S(2)}) copy-start(s32[256]{0:T(256)} %param.9) | copy-start | bytes 3076
  1.3 0.7 %copy-start.3 = (s32[256]{0:T(256)S(1)}, s32[256]{0:T(256)}, u32[]{:S(2)}) copy-start(s32[256]{0:T(256)} %param.11) | copy-start | bytes 3076
  1.3 0.7 %copy-start.1 = (f32[256]{0:T(256)S(1)}, f32[256]{0:T(256)}, u32[]{:S(2)}) copy-start(f32[256]{0:T(256)} %param.8) | copy-start | bytes 3076
  1.3 0.7 %copy-start.4 = (f32[16]{0:T(128)S(1)}, f32[16]{0:T(128)}, u32[]{:S(2)}) copy-start(f32[16]{0:T(128)} %weight_ref.1) | copy-start | bytes 196
  2.0 1.0 %copy-start = (bf16[256,1024]{1,0:T(8,128)(2,1)S(1)}, bf16[256,1024]{1,0:T(8,128)(2,1)}, u32[]{:S(2)}) copy-start(bf16[256,1024]{1,0:T(8,128)(2,1)} %embeds_hbm.1) | copy-start | bytes 1572868

commit v3 on v2

--- a/solution.py
+++ b/solution.py
@@ -7,6 +7,7 @@
 from jax.sharding import PartitionSpec as P
 
 RIDGE = 0.1
+VMEM_BYTES = 67043328
 LANES = 128
 MESH = pl.DeviceIdType.MESH
 
@@ -24,21 +25,29 @@
 def kernel(
     sizes,
     embeds_hbm,
+    quality_hbm,
+    domain_hbm,
+    dest_hbm,
+    weight_hbm,
+    counts_hbm,
+    winners_hbm,
+    recv,
+    gain_ref,
+    chol_ref,
+    embeds,
     quality_ref,
     domain_ref,
     dest_ref,
     weight_ref,
     counts_ref,
     winners_ref,
-    recv,
-    result_ref,
-    embeds,
     send,
     send_quality,
     recv_quality,
     send_winner,
     recv_winner,
     load_sem,
+    fact_sem,
     send_sem,
     recv_sem,
     quality_sem,
@@ -57,9 +66,24 @@
     my_group = me // group
     my_local = me % group
 
+    barrier = pltpu.get_barrier_semaphore()
+    loads = [
+        pltpu.make_async_copy(source, held, fact_sem.at[i])
+        for i, (source, held) in enumerate(
+            (
+                (quality_hbm, quality_ref),
+                (domain_hbm, domain_ref),
+                (dest_hbm, dest_ref),
+                (weight_hbm, weight_ref),
+                (counts_hbm, counts_ref),
+                (winners_hbm, winners_ref),
+            )
+        )
+    ]
+    for load in loads:
+        load.start()
     load = pltpu.make_async_copy(embeds_hbm, embeds, load_sem)
     load.start()
-    barrier = pltpu.get_barrier_semaphore()
 
     @pl.loop(1, shards)
     def _(k):
@@ -70,6 +94,9 @@
             device_id=(peer // pair_size, peer % pair_size),
             device_id_type=MESH,
         )
+
+    for fact_load in loads:
+        fact_load.wait()
 
     dest = dest_ref[...]
     row = lax.broadcasted_iota(jnp.int32, (1, slots), 1)
@@ -187,14 +214,11 @@
             device_id_type=MESH,
         ).start()
 
-    @pl.loop(0, group)
-    def _(k):
-        for bits in range(groups - 1, 0, -1):
+    middle = groups // 2
+    for bits in [middle, *(b for b in range(1, groups) if b != middle), 0]:
+        @pl.loop(0 if bits else 1, group)
+        def _(k):
             send_rows(bits, k)
-
-        @pl.when(k > 0)
-        def _():
-            send_rows(0, k)
 
     own_rows.start()
     own_quality.start()
@@ -314,8 +338,8 @@
             ) / roots[t]
             entries.append(entry)
             gain = gain - entry * entry
-            result_ref[t : t + 1, span] = entry
-        result_ref[steps : steps + 1, span] = gain
+            chol_ref[t : t + 1, span] = entry
+        gain_ref[:, span] = gain
 
     others = recv_winner.at[0, pl.ds(0, spread_size - 1)]
     pltpu.make_async_copy(others, others, send_sem.at[0]).wait()
@@ -325,12 +349,17 @@
     pltpu.make_async_copy(others, others, send_sem.at[2]).wait()
 
 
-def write_kernel(steps, rows_ref, result_ref, relaid_hbm, gain_ref, chol_ref, sem):
-    copy = pltpu.make_async_copy(rows_ref, relaid_hbm, sem)
-    copy.start()
-    gain_ref[...] = result_ref[steps : steps + 1]
-    chol_ref[...] = result_ref[:steps]
-    copy.wait()
+def write_kernel(rows, gain, chol, rows_hbm, gain_hbm, chol_hbm, sem):
+    copies = [
+        pltpu.make_async_copy(held, out, sem.at[i])
+        for i, (held, out) in enumerate(
+            ((rows, rows_hbm), (gain, gain_hbm), (chol, chol_hbm))
+        )
+    ]
+    for copy in copies:
+        copy.start()
+    for copy in copies:
+        copy.wait()
 
 
 def body(embeds, quality, domain_ids, domain_weight, dest, counts, winners):
@@ -343,26 +372,33 @@
     balanced = shards * per_pair
     groups = balanced // LANES
     vmem = pl.BlockSpec(memory_space=pltpu.VMEM)
-    smem = pl.BlockSpec(memory_space=pltpu.SMEM)
     hbm = pl.BlockSpec(memory_space=pltpu.HBM)
     dma = pltpu.SemaphoreType.DMA
     folds = width // LANES
-    rows, result = pl.pallas_call(
+    rows, gain, chol = pl.pallas_call(
         functools.partial(kernel, (pair_size, shards, slots, width, steps, domains)),
         out_shape=(
             pltpu.VMEM((shards, per_pair, width), jnp.bfloat16),
-            pltpu.VMEM((8, balanced), jnp.float32),
+            pltpu.VMEM((1, balanced), jnp.float32),
+            pltpu.VMEM((steps, balanced), jnp.float32),
         ),
-        in_specs=[hbm, vmem, vmem, vmem, smem, smem, smem],
-        out_specs=(vmem, vmem),
+        in_specs=[hbm] * 7,
+        out_specs=(vmem, vmem, vmem),
         scratch_shapes=[
             pltpu.VMEM((slots, width), jnp.bfloat16),
+            pltpu.VMEM((1, slots), jnp.float32),
+            pltpu.VMEM((1, slots), jnp.int32),
+            pltpu.VMEM((1, slots), jnp.int32),
+            pltpu.SMEM((domains,), jnp.float32),
+            pltpu.SMEM((1,), jnp.int32),
+            pltpu.SMEM((steps,), jnp.int32),
             pltpu.VMEM((shards, per_pair, width), jnp.bfloat16),
             pltpu.VMEM((shards, 1, LANES), jnp.float32),
             pltpu.VMEM((shards, 1, LANES), jnp.float32),
             pltpu.VMEM((folds, LANES), jnp.bfloat16),
             pltpu.VMEM((pair_size, shards // pair_size, folds, LANES), jnp.bfloat16),
             dma,
+            dma((6,)),
             dma((3,)),
             dma((groups,)),
             dma((groups,)),
@@ -370,7 +406,7 @@
             dma((2, pair_size - 1)),
         ],
         compiler_params=pltpu.CompilerParams(
-            collective_id=0, has_side_effects=True, vmem_limit_bytes=24 * 1024 * 1024
+            collective_id=0, has_side_effects=True, vmem_limit_bytes=VMEM_BYTES - 1114112
         ),
         name="relay_select",
     )(
@@ -383,18 +419,18 @@
         winners,
     )
     relaid, gain, chol = pl.pallas_call(
-        functools.partial(write_kernel, steps),
+        write_kernel,
         out_shape=(
             jax.ShapeDtypeStruct((shards, per_pair, width), jnp.bfloat16),
             jax.ShapeDtypeStruct((1, balanced), jnp.float32),
             jax.ShapeDtypeStruct((steps, balanced), jnp.float32),
         ),
-        in_specs=[vmem, vmem],
-        out_specs=(hbm, vmem, vmem),
-        scratch_shapes=[dma],
+        in_specs=[vmem] * 3,
+        out_specs=(hbm,) * 3,
+        scratch_shapes=[dma((3,))],
         compiler_params=pltpu.CompilerParams(vmem_limit_bytes=8 * 1024 * 1024),
         name="write_out",
-    )(rows, result)
+    )(rows, gain, chol)
     return relaid.reshape(balanced, width), gain.reshape(balanced), chol
 
 

time: 39.1 us -> 34.6 us (0.88)
  the two profiles are of different devices: /device:TPU:0 before, /device:TPU:9 now
where the time goes in v3:
time: 34.6 us; the launch traced here: 34.4 us
  Pallas kernels  33.1 us (96%)
  between operations  1.29 us (4%)
    pallas_call x1, Pallas kernels, body(): pl.pallas_call(functools.partial(kernel, (pair_size, shards, slots, width...  32.1 us
    pallas_call x1, Pallas kernels, body(): pl.pallas_call(write_kernel, out_shape=(jax.ShapeDtypeStruct((shards, per...  1 us

profile of v3, /device:TPU:9, one launch (start us, length us, event | category | flops | bytes accessed | tf_op | source)
XLA Modules:
  0.0 34.4 jit_solution(4487936938670340554)
XLA Ops:
  1.3 32.1 %relay_select.1 = (bf16[32,16,1024]{2,1,0:T(8,128)(2,1)S(1)}, f32[1,512]{1,0:T(1,128)S(1)}, f32[4,512]{1,0:T(4,128)S(1)}) custom-call(bf16[256,1024]{1,0:T(8,128)(2,1)} %embeds_hbm.1, f32[1,256]{1,0:T(1,128)} %bitcast.5, s32[1,256]{1,0:T(1,128)} %bitcast.6, s32[1,256]{1,0:T(1,128)} %bitcast.7, f32[16]{0:T(128)} %weight_hbm.1, s32[1]{0:T(128)S(6)} %copy.10.counts_hbm, ...), custom_call_target="tpu_custom_call" | custom-call | tf_op jit(solution)/shard_map/relay_select/pallas_call | solution.py:378
  33.4 1.0 %write_out.1 = (bf16[32,16,1024]{2,1,0:T(8,128)(2,1)}, f32[1,512]{1,0:T(1,128)}, f32[4,512]{1,0:T(4,128)}) custom-call(bf16[32,16,1024]{2,1,0:T(8,128)(2,1)S(1)} %get-tuple-element.9.rows, f32[1,512]{1,0:T(1,128)S(1)} %get-tuple-element.10.gain, f32[4,512]{1,0:T(4,128)S(1)} %get-tuple-element.11.chol), custom_call_target="tpu_custom_call" | custom-call | tf_op jit(solution)/shard_map/write_out/pallas_call | solution.py:421

commit v4 on v3

--- a/solution.py
+++ b/solution.py
@@ -53,6 +53,7 @@
     quality_sem,
     winner_sem,
     mate_sem,
+    here_sem,
 ):
     pair_size, shards, slots, width, steps, domains = sizes
     per_pair = 2 * slots // shards
@@ -85,15 +86,21 @@
     load = pltpu.make_async_copy(embeds_hbm, embeds, load_sem)
     load.start()
 
-    @pl.loop(1, shards)
+    def peer_device(bits, k):
+        peer = flip(my_group, bits) * group + (my_local + k) % group
+        return peer, (peer // pair_size, peer % pair_size)
+
+    def greet(semaphore, bits, k):
+        pl.semaphore_signal(
+            semaphore, inc=1, device_id=peer_device(bits, k)[1], device_id_type=MESH
+        )
+
+    for bits in range(groups - 1, 0, -1):
+        greet(barrier, bits, 0)
+
+    @pl.loop(1, group)
     def _(k):
-        peer = (me + k) % shards
-        pl.semaphore_signal(
-            barrier,
-            inc=1,
-            device_id=(peer // pair_size, peer % pair_size),
-            device_id_type=MESH,
-        )
+        greet(barrier, 0, k)
 
     for fact_load in loads:
         fact_load.wait()
@@ -179,24 +186,8 @@
         send_winner, recv_winner.at[me_grp, me_dp], winner_sem.at[0]
     )
 
-    pl.semaphore_wait(barrier, shards - 1)
-
-    @pl.loop(1, spread_size)
-    def _(k):
-        pltpu.make_async_remote_copy(
-            src_ref=send_winner,
-            dst_ref=recv_winner.at[me_grp, me_dp],
-            send_sem=send_sem.at[0],
-            recv_sem=winner_sem.at[0],
-            device_id=((me_dp + k) % spread_size, me_grp),
-            device_id_type=MESH,
-        ).start()
-
-    own_winner.start()
-
     def send_rows(bits, k):
-        peer = flip(my_group, bits) * group + (my_local + k) % group
-        device = (peer // pair_size, peer % pair_size)
+        peer, device = peer_device(bits, k)
         pltpu.make_async_remote_copy(
             src_ref=send_quality.at[peer],
             dst_ref=recv_quality.at[me],
@@ -215,8 +206,30 @@
         ).start()
 
     middle = groups // 2
-    for bits in [middle, *(b for b in range(1, groups) if b != middle), 0]:
-        @pl.loop(0 if bits else 1, group)
+    away = [middle, *(b for b in range(1, groups) if b != middle)]
+    pl.semaphore_wait(barrier, group - 1 + groups - 1)
+    for bits in away:
+        greet(here_sem, bits, 0)
+    for bits in away:
+        send_rows(bits, 0)
+    pl.semaphore_wait(here_sem, groups - 1)
+
+    @pl.loop(1, spread_size)
+    def _(k):
+        pltpu.make_async_remote_copy(
+            src_ref=send_winner,
+            dst_ref=recv_winner.at[me_grp, me_dp],
+            send_sem=send_sem.at[0],
+            recv_sem=winner_sem.at[0],
+            device_id=((me_dp + k) % spread_size, me_grp),
+            device_id_type=MESH,
+        ).start()
+
+    own_winner.start()
+
+    for bits in [*away, 0]:
+
+        @pl.loop(1, group)
         def _(k):
             send_rows(bits, k)
 
@@ -404,6 +417,7 @@
             dma((groups,)),
             dma((1,)),
             dma((2, pair_size - 1)),
+            pltpu.SemaphoreType.REGULAR,
         ],
         compiler_params=pltpu.CompilerParams(
             collective_id=0, has_side_effects=True, vmem_limit_bytes=VMEM_BYTES - 1114112

time: 34.6 us -> 33.3 us (0.962)
  Pallas kernels: 33.1 us -> 31.9 us
    pallas_call x1, Pallas kernels: 32.1 us -> 30.9 us  [body(): pl.pallas_call(functools.partial(kernel, (pair_size, shards, slots, width...]
where the time goes in v4:
time: 33.3 us; the launch traced here: 33.1 us
  Pallas kernels  31.9 us (96%)
  between operations  1.29 us (4%)
    pallas_call x1, Pallas kernels, body(): pl.pallas_call(functools.partial(kernel, (pair_size, shards, slots, width...  30.9 us
    pallas_call x1, Pallas kernels, body(): pl.pallas_call(write_kernel, out_shape=(jax.ShapeDtypeStruct((shards, per...  1 us

profile of v4, /device:TPU:9, one launch (start us, length us, event | category | flops | bytes accessed | tf_op | source)
XLA Modules:
  0.0 33.1 jit_solution(8828864051329707526)
XLA Ops:
  1.3 30.9 %relay_select.1 = (bf16[32,16,1024]{2,1,0:T(8,128)(2,1)S(1)}, f32[1,512]{1,0:T(1,128)S(1)}, f32[4,512]{1,0:T(4,128)S(1)}) custom-call(bf16[256,1024]{1,0:T(8,128)(2,1)} %embeds_hbm.1, f32[1,256]{1,0:T(1,128)} %bitcast.5, s32[1,256]{1,0:T(1,128)} %bitcast.6, s32[1,256]{1,0:T(1,128)} %bitcast.7, f32[16]{0:T(128)} %weight_hbm.1, s32[1]{0:T(128)S(6)} %copy.10.counts_hbm, ...), custom_call_target="tpu_custom_call" | custom-call | tf_op jit(solution)/shard_map/relay_select/pallas_call | solution.py:391
  32.1 1.0 %write_out.1 = (bf16[32,16,1024]{2,1,0:T(8,128)(2,1)}, f32[1,512]{1,0:T(1,128)}, f32[4,512]{1,0:T(4,128)}) custom-call(bf16[32,16,1024]{2,1,0:T(8,128)(2,1)S(1)} %get-tuple-element.9.rows, f32[1,512]{1,0:T(1,128)S(1)} %get-tuple-element.10.gain, f32[4,512]{1,0:T(4,128)S(1)} %get-tuple-element.11.chol), custom_call_target="tpu_custom_call" | custom-call | tf_op jit(solution)/shard_map/write_out/pallas_call | solution.py:435

commit v5 on v4

--- a/solution.py
+++ b/solution.py
@@ -68,6 +68,22 @@
     my_local = me % group
 
     barrier = pltpu.get_barrier_semaphore()
+    def peer_device(bits, k):
+        peer = flip(my_group, bits) * group + (my_local + k) % group
+        return peer, (peer // pair_size, peer % pair_size)
+
+    def greet(semaphore, bits, k):
+        pl.semaphore_signal(
+            semaphore, inc=1, device_id=peer_device(bits, k)[1], device_id_type=MESH
+        )
+
+    for bits in range(groups - 1, 0, -1):
+        greet(barrier, bits, 0)
+
+    @pl.loop(1, group)
+    def _(k):
+        greet(barrier, 0, k)
+
     loads = [
         pltpu.make_async_copy(source, held, fact_sem.at[i])
         for i, (source, held) in enumerate(
@@ -85,22 +101,6 @@
         load.start()
     load = pltpu.make_async_copy(embeds_hbm, embeds, load_sem)
     load.start()
-
-    def peer_device(bits, k):
-        peer = flip(my_group, bits) * group + (my_local + k) % group
-        return peer, (peer // pair_size, peer % pair_size)
-
-    def greet(semaphore, bits, k):
-        pl.semaphore_signal(
-            semaphore, inc=1, device_id=peer_device(bits, k)[1], device_id_type=MESH
-        )
-
-    for bits in range(groups - 1, 0, -1):
-        greet(barrier, bits, 0)
-
-    @pl.loop(1, group)
-    def _(k):
-        greet(barrier, 0, k)
 
     for fact_load in loads:
         fact_load.wait()
@@ -363,11 +363,13 @@
 
 
 def write_kernel(rows, gain, chol, rows_hbm, gain_hbm, chol_hbm, sem):
+    quarter = rows.shape[0] // 4
+    parts = [pl.ds(i * quarter, quarter) for i in range(4)]
+    pairs = [(rows.at[part], rows_hbm.at[part]) for part in parts]
+    pairs += [(gain, gain_hbm), (chol, chol_hbm)]
     copies = [
         pltpu.make_async_copy(held, out, sem.at[i])
-        for i, (held, out) in enumerate(
-            ((rows, rows_hbm), (gain, gain_hbm), (chol, chol_hbm))
-        )
+        for i, (held, out) in enumerate(pairs)
     ]
     for copy in copies:
         copy.start()
@@ -441,7 +443,7 @@
         ),
         in_specs=[vmem] * 3,
         out_specs=(hbm,) * 3,
-        scratch_shapes=[dma((3,))],
+        scratch_shapes=[dma((6,))],
         compiler_params=pltpu.CompilerParams(vmem_limit_bytes=8 * 1024 * 1024),
         name="write_out",
     )(rows, gain, chol)

time: 33.3 us -> 33.4 us (level)
  the two profiles are of different devices: /device:TPU:9 before, /device:TPU:13 now
where the time goes in v5:
time: 33.4 us; the launch traced here: 33.2 us
  Pallas kernels  31.9 us (96%)
  between operations  1.29 us (4%)
    pallas_call x1, Pallas kernels, body(): pl.pallas_call(functools.partial(kernel, (pair_size, shards, slots, width...  30.9 us
    pallas_call x1, Pallas kernels, body(): pl.pallas_call(write_kernel, out_shape=(jax.ShapeDtypeStruct((shards, per...  1.02 us

profile of v5, /device:TPU:13, one launch (start us, length us, event | category | flops | bytes accessed | tf_op | source)
XLA Modules:
  0.0 33.2 jit_solution(13687948166709163178)
XLA Ops:
  1.3 30.9 %relay_select.1 = (bf16[32,16,1024]{2,1,0:T(8,128)(2,1)S(1)}, f32[1,512]{1,0:T(1,128)S(1)}, f32[4,512]{1,0:T(4,128)S(1)}) custom-call(bf16[256,1024]{1,0:T(8,128)(2,1)} %embeds_hbm.1, f32[1,256]{1,0:T(1,128)} %bitcast.5, s32[1,256]{1,0:T(1,128)} %bitcast.6, s32[1,256]{1,0:T(1,128)} %bitcast.7, f32[16]{0:T(128)} %weight_hbm.1, s32[1]{0:T(128)S(6)} %copy.10.counts_hbm, ...), custom_call_target="tpu_custom_call" | custom-call | tf_op jit(solution)/shard_map/relay_select/pallas_call | solution.py:393
  32.2 1.0 %write_out.1 = (bf16[32,16,1024]{2,1,0:T(8,128)(2,1)}, f32[1,512]{1,0:T(1,128)}, f32[4,512]{1,0:T(4,128)}) custom-call(bf16[32,16,1024]{2,1,0:T(8,128)(2,1)S(1)} %get-tuple-element.9.rows, f32[1,512]{1,0:T(1,128)S(1)} %get-tuple-element.10.gain, f32[4,512]{1,0:T(4,128)S(1)} %get-tuple-element.11.chol), custom_call_target="tpu_custom_call" | custom-call | tf_op jit(solution)/shard_map/write_out/pallas_call | solution.py:437
